TPU v7x, 256 devices: a whole 4x4x8 slice. The times are simulated.
256 devices in a mesh: ctx: 128 (over y, x, z), tp: 2 (over core).
Axes of the slice: x: 4, y: 4, z: 8, core: 2. Of those that a mesh axis runs over, the one named last changes fastest.
Arguments:
- hidden: bfloat16 [32768, 4096], P('ctx', 'tp'), may hold values from -6 to 6
- w_query: bfloat16 [4096, 4096], P('ctx', 'tp'), may hold values from -0.09375 to 0.09375
- key_weight: bfloat16 [4096, 256], P('ctx', 'tp'), may hold values from -0.09375 to 0.09375
- value_weight: bfloat16 [4096, 256], P('ctx', 'tp'), may hold values from -0.09375 to 0.09375
- q_gain: float32 [128], replicated, may hold values from 0.5 to 2
- key_norm_gain: float32 [128], replicated, may hold values from 0.5 to 2
- earlier_keys: bfloat16 [131072, 256], P('ctx', 'tp'), may hold values from -288 to 288
- earlier_values: bfloat16 [131072, 256], P('ctx', 'tp'), may hold values from -6 to 6
- counts: int32 [64], replicated, may hold values from 1 to 16, as said below
- place: int32 [64, 16], replicated, may hold values from 0 to 15, as said below
Outputs:
- attended: bfloat16 [32768, 4096], P('ctx', 'tp')
- new_keys: bfloat16 [32768, 256], P('ctx', 'tp')
- new_values: bfloat16 [32768, 256], P('ctx', 'tp')
Inputs may be any that keep to these rules, and one draw needn't show every extreme that they name: `counts`: 16 for one trajectory and 1 for another in every draw; most trajectories have few blocks. `place`: each row orders all 16 slots of the trajectory; the slots after the first counts[b] hold stale data.
All inputs are finite; a program needn't handle non-finite values.
Results may differ from a plain program's by a relative error of at most 0.007.
Values may be sent and summed in bfloat16 or wider, within the bound.
A program may use at most 64 MiB of HBM per device.

v0:
```python
import math

import jax
import jax.numpy as jnp
from jax import lax
from jax.sharding import PartitionSpec as P

HEAD_SIZE = 128
BLOCK_TOKENS = 128


def from_partner(value, axis, apart):
    mask = 2**apart
    pairs = [(source, source ^ mask) for source in range(lax.axis_size(axis))]
    return lax.ppermute(value, axis, pairs)


def normalize_and_turn(values, gain, token_position):
    width = values.shape[-1]
    half = width // 2
    scaled = values * lax.rsqrt(jnp.mean(values * values, axis=-1, keepdims=True) + 1e-06) * gain
    freq = jnp.exp(jnp.arange(half, dtype=jnp.float32) * (-2.0 / width) * math.log(1000000.0))
    angle = token_position.astype(jnp.float32)[:, None] * freq[None, :]
    cosine = jnp.cos(angle)[:, None, :]
    sine = jnp.sin(angle)[:, None, :]
    leading_index = scaled[..., :half]
    second = scaled[..., half:]
    return jnp.concatenate(
        [leading_index * cosine - second * sine, second * cosine + leading_index * sine], axis=-1
    )


def in_order(mine, theirs, lower):
    return jnp.where(
        lower, jnp.concatenate([mine, theirs], axis=0), jnp.concatenate([theirs, mine], axis=0)
    )


def on_device(
    hidden,
    w_query,
    key_weight,
    value_weight,
    q_gain,
    key_norm_gain,
    earlier_keys,
    earlier_values,
    counts,
    place,
):
    lower = lax.axis_index("ctx") % 2 == 0
    traj_id = lax.axis_index("ctx") // 2
    whole = lax.all_gather(hidden, "tp", axis=1, tiled=True)
    tok_rows = whole.shape[0]

    def add_rows(piece):
        return jnp.dot(whole, piece, preferred_element_type=jnp.float32)

    query = add_rows(lax.all_gather(w_query, "ctx", axis=0, tiled=True))
    key_projected = add_rows(lax.all_gather(key_weight, "ctx", axis=0, tiled=True))
    value_projected = add_rows(lax.all_gather(value_weight, "ctx", axis=0, tiled=True))
    heads_q = w_query.shape[1] // HEAD_SIZE
    heads_kv = key_weight.shape[1] // HEAD_SIZE
    count = lax.dynamic_index_in_dim(counts, traj_id, 0, keepdims=False)
    offsets = lax.axis_index("ctx") % 2 * tok_rows + jnp.arange(tok_rows, dtype=jnp.int32)
    token_position = count * BLOCK_TOKENS + offsets
    rotated = normalize_and_turn(
        query.reshape(tok_rows, heads_q, HEAD_SIZE), q_gain, token_position
    ).astype(jnp.bfloat16)
    keys_mine = (
        normalize_and_turn(
            key_projected.reshape(tok_rows, heads_kv, HEAD_SIZE), key_norm_gain, token_position
        )
        .astype(jnp.bfloat16)
        .reshape(tok_rows, heads_kv * HEAD_SIZE)
    )
    values_mine = value_projected.astype(jnp.bfloat16)
    other_ck, other_cv, keys_other, values_other = from_partner(
        (earlier_keys, earlier_values, keys_mine, values_mine), "ctx", 0
    )
    keys_all = jnp.concatenate(
        [in_order(earlier_keys, other_ck, lower), in_order(keys_mine, keys_other, lower)], axis=0
    )
    vals_all = jnp.concatenate(
        [in_order(earlier_values, other_cv, lower), in_order(values_mine, values_other, lower)],
        axis=0,
    )
    slot_total = place.shape[1]
    cache_rows = slot_total * BLOCK_TOKENS
    order = lax.dynamic_index_in_dim(place, traj_id, 0, keepdims=False)
    used = jnp.arange(slot_total, dtype=jnp.int32) < count
    live = jnp.any(
        (order[:, None] == jnp.arange(slot_total, dtype=jnp.int32)[None, :]) & used[:, None], axis=0
    )
    live_tok = jnp.repeat(live, BLOCK_TOKENS)
    stretch_pos = jnp.arange(2 * tok_rows, dtype=jnp.int32)
    query_group = heads_q // heads_kv
    rows_total = query_group * tok_rows
    block_rows = min(rows_total, 512)
    block_count = rows_total // block_rows
    starts = jnp.arange(block_count, dtype=jnp.int32) * block_rows
    query_rows = jnp.transpose(rotated, (1, 0, 2)).reshape(block_count, block_rows, HEAD_SIZE)

    def attend(operands):
        block, begin = operands
        token = (begin + jnp.arange(block_rows, dtype=jnp.int32)) % tok_rows
        own_pos = lax.axis_index("ctx") % 2 * tok_rows + token
        score = lax.dot_general(
            block, keys_all, (((1,), (1,)), ((), ())), preferred_element_type=jnp.float32
        ) * HEAD_SIZE ** (-0.5)
        allowed = jnp.concatenate(
            [
                jnp.broadcast_to(live_tok[None, :], (block_rows, cache_rows)),
                stretch_pos[None, :] <= own_pos[:, None],
            ],
            axis=1,
        )
        score = jnp.where(allowed, score, -jnp.inf)
        top = jnp.max(score, axis=-1, keepdims=True)
        weight = jnp.exp(score - top)
        total = jnp.sum(weight, axis=-1, keepdims=True)
        mixed = (
            jnp.dot(weight.astype(jnp.bfloat16), vals_all, preferred_element_type=jnp.float32)
            / total
        )
        return mixed.astype(jnp.bfloat16)

    result = lax.map(attend, (query_rows, starts))
    outputs = jnp.transpose(result.reshape(query_group, tok_rows, HEAD_SIZE), (1, 0, 2))
    attended = outputs.reshape(tok_rows, heads_q * HEAD_SIZE)
    return (attended, keys_mine, values_mine)


def solution(mesh):
    placed = (
        P("ctx", "tp"),
        P("ctx", "tp"),
        P("ctx", "tp"),
        P("ctx", "tp"),
        P(),
        P(),
        P("ctx", "tp"),
        P("ctx", "tp"),
        P(),
        P(),
    )
    return jax.shard_map(
        on_device,
        mesh=mesh,
        in_specs=placed,
        out_specs=(P("ctx", "tp"), P("ctx", "tp"), P("ctx", "tp")),
        check_vma=False,
    )
```

profile of v0, /device:TPU:1, one launch (start us, length us, event | category | flops | bytes accessed | tf_op | source)
XLA Modules:
  0.0 450.9 jit_solution(13506586590148056657)
XLA Ops:
  7.2 0.7 all-gather.9.cloned.1.call-update
  8.0 0.7 all-gather.5.cloned.1.call-update
  8.7 0.7 all-gather.11.cloned.1.call-update
  10.0 2.6 collective-permute-start
  12.6 1.2 dynamic_slice.25
  15.1 0.7 iota_compare_fusion.2
  16.6 1.2 collective-permute-done
  17.8 1.2 maximum_select_fusion
  19.0 4.4 collective-permute-done.2
  23.6 90.1 %all-gather.9.cloned.1.call-done = bf16[4096,128]{1,0:T(8,128)(2,1)} async-done(((bf16[32,128]{1,0:T(8,128)(2,1)}), bf16[4096,128]{1,0:T(8,128)(2,1)}) %all-gather.9.cloned.1.call-update) | async-done | bytes 1048592 | tf_op jit(solution)/shard_map/all_gather | solution.py:60
  113.7 21.4 %all-gather.5.cloned.1.call-done = bf16[256,4096]{1,0:T(8,128)(2,1)} async-done(((bf16[256,2048]{1,0:T(8,128)(2,1)}), bf16[256,4096]{1,0:T(8,128)(2,1)}) %all-gather.5.cloned.1.call-update) | async-done | bytes 2097168 | tf_op jit(solution)/shard_map/all_gather | solution.py:53
  135.2 2.8 multiply_reduce_fusion.1
  138.0 0.7 multiply_bitcast_fusion
  139.7 1.0 collective-permute-start.1
  140.7 96.9 %all-gather.11.cloned.1.call-done = bf16[4096,128]{1,0:T(8,128)(2,1)} async-done(((bf16[32,128]{1,0:T(8,128)(2,1)}), bf16[4096,128]{1,0:T(8,128)(2,1)}) %all-gather.11.cloned.1.call-update) | async-done | bytes 1048592 | tf_op jit(solution)/shard_map/all_gather | solution.py:61
  237.6 2.1 convolution_convert_fusion
  239.7 1.6 copy.49
  241.3 0.7 copy.50
  242.0 1.2 collective-permute-start.3
  243.2 1.6 maximum_select_fusion.2
  244.8 1.7 copy.45
  246.5 1.6 maximum_select_fusion.3
  248.1 1.7 copy.47
  249.7 1.8 pad_maximum_fusion
  251.5 0.9 pad_maximum_fusion.1
  252.5 141.8 %all-gather.7.cloned.1.call-done = bf16[4096,2048]{1,0:T(8,128)(2,1)} async-done(((bf16[32,2048]{1,0:T(8,128)(2,1)}), bf16[4096,2048]{1,0:T(8,128)(2,1)}) %all-gather.7.cloned.1.call-update) | async-done | bytes 16777232 | tf_op jit(solution)/shard_map/all_gather | solution.py:59
  394.3 8.2 %convolution_bitcast_fusion = f32[32,8,16,128]{3,1,2,0:T(8,128)S(1)} fusion(bf16[256,4096]{1,0:T(8,128)(2,1)S(1)} %copy-done.1, bf16[4096,2048]{1,0:T(8,128)(2,1)} %all-gather.7.cloned.1.call-done), kind=kOutput, calls=%fused_computation.26 | convolution fusion | flops 4294967296 | bytes 20971520 | tf_op jit(solution)/shard_map/dot_general | solution.py:57
  403.7 0.9 multiply_multiply_fusion
  404.6 0.8 subtract_convert_fusion
  406.8 35.5 %while.14 = (s32[]{:T(128)}, bf16[8,512,128]{2,1,0:T(8,128)(2,1)S(1)}, s32[8]{0:T(128)S(1)}, bf16[8,512,128]{2,1,0:T(8,128)(2,1)S(1)}, bf16[2560,128]{1,0:T(8,12...) while((s32[]{:T(128)}, ...), condition=%wide.region_6.7_spmd.clone, body=%wide.region_3.6_spmd.clone.sunk | while | flops 681973248 | bytes 17850196 | solution.py:128
  407.4 0.7 fusion.57
  408.4 1.1 fusion.58
  409.4 0.8 fusion.59
  410.3 1.0 fusion.60
  411.9 0.7 fusion.57
  412.8 1.1 fusion.58
  413.9 0.8 fusion.59
  414.7 1.0 fusion.60
  416.3 0.7 fusion.57
  417.3 1.1 fusion.58
  418.3 0.8 fusion.59
  419.2 1.0 fusion.60
  420.8 0.7 fusion.57
  421.7 1.1 fusion.58
  422.8 0.8 fusion.59
  423.6 1.0 fusion.60
  425.2 0.7 fusion.57
  426.2 1.1 fusion.58
  427.2 0.8 fusion.59
  428.1 1.0 fusion.60
  429.7 0.7 fusion.57
  430.6 1.1 fusion.58
  431.7 0.8 fusion.59
  432.5 1.0 fusion.60
  434.1 0.7 fusion.57
  435.1 1.1 fusion.58
  436.1 0.8 fusion.59
  437.0 1.0 fusion.60
  438.5 0.7 fusion.57
  439.5 1.1 fusion.58
  440.6 0.8 fusion.59
  441.4 1.0 fusion.60
  442.4 0.7 copy.48
  443.1 1.2 copy.55
  (76 shorter events, 12.9 us)
Async XLA Ops:
  7.2 8.6 %copy-start = (s32[64,16]{0,1:T(8,128)S(1)}, s32[64,16]{0,1:T(8,128)}, u32[]{:S(2)}) copy-start(s32[64,16]{0,1:T(8,128)} %param.21) | copy-start | bytes 12292
  7.2 16.3 %copy-start.4 = (bf16[1024,128]{1,0:T(8,128)(2,1)S(1)}, bf16[1024,128]{1,0:T(8,128)(2,1)}, u32[]{:S(2)}) copy-start(bf16[1024,128]{1,0:T(8,128)(2,1)} %param.19) | copy-start | bytes 786436
  7.2 106.5 %all-gather.9.cloned.1.call-start = ((), (), s32[]{:S(2)}) async-start(), calls=%async_computation.2 | async-start | bytes 1056768 | tf_op jit(solution)/shard_map/all_gather | solution.py:60
  7.9 127.2 %all-gather.5.cloned.1.call-start = ((), (), s32[]{:S(2)}) async-start(), calls=%async_computation | async-start | bytes 3145728 | tf_op jit(solution)/shard_map/all_gather | solution.py:53
  8.7 229.0 %all-gather.11.cloned.1.call-start = ((), (), s32[]{:S(2)}) async-start(), calls=%async_computation.3 | async-start | bytes 1056768 | tf_op jit(solution)/shard_map/all_gather | solution.py:61
  9.4 384.9 %all-gather.7.cloned.1.call-start = ((), (), s32[]{:S(2)}) async-start(), calls=%async_computation.1 | async-start | bytes 16908288 | tf_op jit(solution)/shard_map/all_gather | solution.py:59
  10.0 7.8 %collective-permute-start = (bf16[1024,128]{1,0:T(8,128)(2,1)}, bf16[1024,128]{1,0:T(8,128)(2,1)S(1)}, u32[]{:S(2)}, u32[]{:S(2)}) collective-permute-start(bf16[1024,128]{1,0:T(8,128)(2,1)} %param.18), channel_id=1, source_target_pairs={{0,2},{2,0},{4,6},{6,4},{8,10},{10,8},{12,14},{14,12},{16,18},{18,... | collective-permute-start | bytes 786440 | tf_op jit(solution)/shard_map/ppermute | solution.py:15
  12.5 10.9 %collective-permute-start.2 = (bf16[1024,128]{1,0:T(8,128)(2,1)}, bf16[1024,128]{1,0:T(8,128)(2,1)S(1)}, u32[]{:S(2)}, u32[]{:S(2)}) collective-permute-start(bf16[1024,128]{1,0:T(8,128)(2,1)} %param.19), channel_id=1, source_target_pairs={{0,2},{2,0},{4,6},{6,4},{8,10},{10,8},{12,14},{14,12},{16,18},{18,... | collective-permute-start | bytes 786440 | tf_op jit(solution)/shard_map/ppermute | solution.py:15
  14.5 4.5 copy-start.5
  135.2 3.6 copy-start.6
  135.2 102.5 %copy-start.1 = (bf16[256,4096]{1,0:T(8,128)(2,1)S(1)}, bf16[256,4096]{1,0:T(8,128)(2,1)}, u32[]{:S(2)}) copy-start(bf16[256,4096]{1,0:T(8,128)(2,1)} %all-gather.5.cloned.1.call-done) | copy-start | bytes 6291460
  139.7 103.5 %collective-permute-start.1 = (bf16[256,128]{0,1:T(8,128)(2,1)}, bf16[256,128]{0,1:T(8,128)(2,1)}, u32[]{:S(2)}, u32[]{:S(2)}) collective-permute-start(bf16[256,128]{0,1:T(8,128)(2,1)} %pad_maximum_fusion.2), channel_id=1, source_target_pairs={{0,2},{2,0},{4,6},{6,4},{8,10},{10,8},{12,14},{14,12},{16,18},{18,... | collective-permute-start | bytes 196616 | tf_op jit(solution)/shard_map/ppermute | solution.py:15
  242.0 4.4 collective-permute-start.3
  402.9 0.8 copy-start.7
  405.4 1.2 copy-start.2
  405.4 1.4 copy-start.3
  405.4 1.4 copy-start.8
Sparse Core Ops, SparseCore 0:
  11.4 102.2 all-gather.8
  115.5 19.6 all-gather.4
  138.6 99.0 all-gather.10
  241.1 153.1 all-gather.6
where the time goes:
time: 451 us
  waiting for transfers between devices  358 us (79%)
  matrix products  29.2 us (6%)
  other arithmetic  27.5 us (6%)
  local copies, waits for them, and re-layouts  15.7 us (3%)
  between operations  14.7 us (3%)
  starting transfers between devices  4.99 us (1%)
    all_gather x1, waiting for transfers between devices, on_device(): query = add_rows(lax.all_gather(w_query, 'ctx', axis=0, tiled=True))  142 us
    all_gather x1, waiting for transfers between devices, on_device(): lax.all_gather(value_weight, 'ctx', axis=0, tiled=True)  96.9 us
    all_gather x1, waiting for transfers between devices, on_device(): lax.all_gather(key_weight, 'ctx', axis=0, tiled=True)  90.1 us
    all_gather x1, waiting for transfers between devices, on_device(): whole = lax.all_gather(hidden, 'tp', axis=1, tiled=True)  21.4 us
    dot_general x3, matrix products, add_rows(): return jnp.dot(whole, piece, preferred_element_type=jnp.float32)  13.1 us
  transfers between devices with their start and end apart: 8, of which 6 were waited for; matrix products, arithmetic and copies ran while one was open for 5% of the time, Pallas kernels for 0%

commit v1 on v0

v1 whole, which is shorter than its diff:
```python
import functools
import math

import jax
import jax.numpy as jnp
from jax import lax
from jax.experimental import pallas as pl
from jax.experimental.pallas import tpu as pltpu
from jax.sharding import PartitionSpec as P

MESH = pl.DeviceIdType.MESH
HEAD = 128
BLOCK = 128
TOK = 256
NY, NX, NZ = 4, 4, 8
SLOTS = 16
CACHE = SLOTS * BLOCK
KEYS = CACHE + 2 * TOK
FACTOR = HEAD**-0.5 * math.log2(math.e)
NEG = -1e30


def kernel(
    counts, place, hid, wq, kw, vw, qg, kg, ck, cv,
    att, nk, nv,
    H, W, KC, VC, KN, VN, KM, VM, QS, QA, COS, SIN, TRI, O,
    local_sem, out_sem,
    p0_s, p0_r, h_s, h_r, c_s, c_r, kv_s, kv_r, za_s, za_r, xa_s, xa_r, xb_s, xb_r, zb_s, zb_r, q_s, q_r,
):
    i = lax.axis_index("ctx")
    c = lax.axis_index("tp")
    y, x, z = i // (NX * NZ), (i // NZ) % NX, i % NZ
    zp = z % 2
    sent = []

    def ym(k):
        return (y + k + NY) % NY

    def xm(k):
        return (x + k + NX) % NX

    def zm(k):
        return (z + k + NZ) % NZ

    def at(dy=0, dx=0, dz=0):
        return (ym(dy) * (NX * NZ) + xm(dx) * NZ + zm(dz), c)

    other_core = (i, 1 - c)
    pair = (i + 1 - 2 * zp, c)

    def send(src, dst, s, r, device):
        copy = pltpu.make_async_remote_copy(
            src_ref=src, dst_ref=dst, send_sem=s, recv_sem=r, device_id=device, device_id_type=MESH
        )
        copy.start()
        sent.append(copy)

    def arrived(dst, s, r):
        pltpu.make_async_remote_copy(
            src_ref=dst, dst_ref=dst, send_sem=s, recv_sem=r, device_id=other_core, device_id_type=MESH
        ).wait_recv()

    local = []

    def bring(src, dst):
        copy = pltpu.make_async_copy(src, dst, local_sem.at[len(local)])
        copy.start()
        local.append(copy)

    def columns(yb, g):
        return pl.ds(pl.multiple_of(yb * 512 + (g - 1) * 256, 256), 256)

    bring(wq.at[:, columns(y, 1)], W.at[1, y, x, z])
    bring(kw, W.at[0, y, x, z, :, pl.ds(0, 128)])
    bring(vw, W.at[0, y, x, z, :, pl.ds(128, 128)])
    bring(wq.at[:, columns(y, 2)], W.at[2, y, x, z])
    bring(hid, H.at[y, c])
    bring(ck, KC.at[zp])
    bring(cv, VC.at[zp])

    barrier = pltpu.get_barrier_semaphore()
    for device in (at(dy=1), at(dy=-1), at(dy=2), at(dx=1), at(dx=-1), at(dz=1), at(dz=-1), other_core):
        pl.semaphore_signal(barrier, inc=1, device_id=device, device_id_type=MESH)
    pl.semaphore_wait(barrier, 8)

    steps_y = (1, -1, 2)
    for g in (1, 0, 2):
        for n, dy in enumerate(steps_y):
            if g == 0:
                for m, part in enumerate((kw, vw)):
                    send(part, W.at[0, y, x, z, :, pl.ds(128 * m, 128)], p0_s.at[n, 2 + m], p0_r.at[n, 2 + m], at(dy=dy))
            else:
                send(wq.at[:, columns(ym(dy), g)], W.at[g, y, x, z], p0_s.at[n, g - 1], p0_r.at[n, g - 1], at(dy=dy))

    def own_rows(g):
        for n, dy in enumerate(steps_y):
            if g == 0:
                for m in range(2):
                    arrived(W.at[0, ym(-dy), x, z, :, pl.ds(128 * m, 128)], p0_s.at[n, 2 + m], p0_r.at[n, 2 + m])
            else:
                arrived(W.at[g, ym(-dy), x, z], p0_s.at[n, g - 1], p0_r.at[n, g - 1])

    def half(n):
        return pl.ds(128 * n, 128)

    for n in (0, 1):
        send(hid.at[half(n)], H.at[y, c, half(n)], h_s.at[0, n], h_r.at[0, n], at(dy=1))
        send(hid.at[half(1 - n)], H.at[y, c, half(1 - n)], h_s.at[1, 1 - n], h_r.at[1, 1 - n], at(dy=-1))
    send(hid, H.at[y, c], c_s.at[0], c_r.at[0], other_core)

    def h_arrived(d, n):
        arrived(H.at[ym(-1 if d == 0 else 1), c, half(n)], h_s.at[d, n], h_r.at[d, n])

    def h_forward(d):
        yb = ym(-1 if d == 0 else 1)
        send(H.at[yb, c, half(d)], H.at[yb, c, half(d)], h_s.at[2, d], h_r.at[2, d], at(dy=1 if d == 0 else -1))

    def h_far_arrived(d):
        arrived(H.at[ym(2), c, half(d)], h_s.at[2, d], h_r.at[2, d])

    def h_to_core(yb, slot, rows=None):
        ref = H.at[yb, c] if rows is None else H.at[yb, c, rows]
        send(ref, ref, c_s.at[slot], c_r.at[slot], other_core)

    def h_from_core(yb, slot, rows=None):
        ref = H.at[yb, 1 - c] if rows is None else H.at[yb, 1 - c, rows]
        arrived(ref, c_s.at[slot], c_r.at[slot])

    def order(j):
        return zm((0, -1, 1, -2, 2, -3, 3, 4)[j])

    def a_block(g, xx, zz, hop=1, d=0):
        if hop == 4:
            return W.at[g, pl.ds(2 * d, 2), xx, zz]
        return W.at[g, :, xx, zz]

    def a_zsend(g, d, hop):
        sign = 1 - 2 * d
        ref = a_block(g, x, zm(-sign * (hop - 1)), hop, d)
        send(ref, ref, za_s.at[g - 1, d, hop - 1], za_r.at[g - 1, d, hop - 1], at(dz=sign))

    def a_zwait(g, d, hop):
        sign = 1 - 2 * d
        arrived(a_block(g, x, zm(-sign * hop), hop, d), za_s.at[g - 1, d, hop - 1], za_r.at[g - 1, d, hop - 1])

    def a_xsend(g, j):
        for d in (0, 1):
            ref = a_block(g, x, order(j))
            send(ref, ref, xa_s.at[g - 1, d, j], xa_r.at[g - 1, d, j], at(dx=1 - 2 * d))

    def a_xwait(g, d, j):
        arrived(a_block(g, xm(2 * d - 1), order(j)), xa_s.at[g - 1, d, j], xa_r.at[g - 1, d, j])

    def a_xforward(g, j):
        d = j % 2
        a_xwait(g, d, j)
        ref = a_block(g, xm(2 * d - 1), order(j))
        send(ref, ref, xa_s.at[g - 1, 2, j], xa_r.at[g - 1, 2, j], at(dx=1 - 2 * d))

    def a_step(g, n):
        if n == 0:
            own_rows(g)
            a_zsend(g, 0, 1)
            a_zsend(g, 1, 1)
            a_xsend(g, 0)
        elif n <= 3:
            for d in (0, 1):
                a_zwait(g, d, n)
                a_zsend(g, d, n + 1)
            for d in (0, 1):
                a_xsend(g, 2 * n - 1 + d)
            for j in ((0,), (1, 2), (3, 4))[n - 1]:
                a_xforward(g, j)
        elif n == 4:
            a_zwait(g, 0, 4)
            a_zwait(g, 1, 4)
            a_xsend(g, 7)
            a_xforward(g, 5)
            a_xforward(g, 6)
        elif n == 5:
            a_xforward(g, 7)
        else:
            for j in range(8):
                a_xwait(g, 1 - j % 2, j)
                arrived(a_block(g, xm(2), order(j)), xa_s.at[g - 1, 2, j], xa_r.at[g - 1, 2, j])

    far = (0, -1, 1, 2)

    def b_zsend(n, hop):
        for d in (0, 1):
            sign = 1 - 2 * d
            ref = a_block(0, xm(far[n]), zm(-sign * (hop - 1)), hop, d)
            send(ref, ref, zb_s.at[n, d, hop - 1], zb_r.at[n, d, hop - 1], at(dz=sign))

    def b_zwait(n, hop):
        for d in (0, 1):
            sign = 1 - 2 * d
            arrived(a_block(0, xm(far[n]), zm(-sign * hop), hop, d), zb_s.at[n, d, hop - 1], zb_r.at[n, d, hop - 1])

    def b_step(n):
        if n == 0:
            own_rows(0)
            for d in (0, 1):
                ref = a_block(0, x, z)
                send(ref, ref, xb_s.at[d], xb_r.at[d], at(dx=1 - 2 * d))
            b_zsend(0, 1)
        elif n == 1:
            for d in (0, 1):
                arrived(a_block(0, xm(2 * d - 1), z), xb_s.at[d], xb_r.at[d])
                ref = a_block(0, xm(2 * d - 1), z, 4, d)
                send(ref, ref, xb_s.at[2 + d], xb_r.at[2 + d], at(dx=1 - 2 * d))
            b_zsend(1, 1)
            b_zsend(2, 1)
        elif n == 2:
            for d in (0, 1):
                arrived(a_block(0, xm(2), z, 4, d), xb_s.at[2 + d], xb_r.at[2 + d])
            b_zsend(3, 1)
        elif n <= 5:
            for m in range(4):
                b_zwait(m, n - 2)
                b_zsend(m, n - 1)
        else:
            for m in range(4):
                b_zwait(m, 4)

    def trajectory(yb):
        return (yb * (NX * NZ) + x * NZ + z) // 2

    lane = lax.broadcasted_iota(jnp.int32, (TOK, HEAD), 1)
    freq = jnp.exp((lane % 64).astype(jnp.float32) * (-2.0 / HEAD) * math.log(1000000.0))

    def tables(yb):
        start = counts[trajectory(yb)] * BLOCK + zp * TOK
        pos = (start + lax.broadcasted_iota(jnp.int32, (TOK, HEAD), 0)).astype(jnp.float32)
        angle = pos * freq
        COS[yb] = jnp.cos(angle)
        SIN[yb] = jnp.where(lane < 64, -1.0, 1.0) * jnp.sin(angle)

    def turned(v, gain, yb):
        v = v * lax.rsqrt(jnp.mean(v * v, axis=-1, keepdims=True) + 1e-06) * gain
        return (v * COS[yb] + pltpu.roll(v, 64, 1) * SIN[yb]).astype(jnp.bfloat16)

    def project(yb, g):
        rows = NY // 2 * NX * NZ * 32
        low = jnp.dot(H[yb, 0], W[g, 0:2].reshape(rows, 256), preferred_element_type=jnp.float32)
        high = jnp.dot(H[yb, 1], W[g, 2:4].reshape(rows, 256), preferred_element_type=jnp.float32)
        return low + high

    def queries(yb, g):
        out = project(yb, g)
        for h in (0, 1):
            QS[yb, 2 * (g - 1) + h] = turned(out[:, h * HEAD : (h + 1) * HEAD], qg[...], yb)

    def own_queries(g):
        queries(y, g)
        for h in (0, 1):
            QA[4 * y + 2 * (g - 1) + h] = QS[y, 2 * (g - 1) + h]

    def q_send(n, g):
        dy = steps_y[n]
        heads = pl.ds(2 * (g - 1), 2)
        send(QS.at[ym(dy), heads], QA.at[pl.ds(4 * y + 2 * (g - 1), 2)], q_s.at[n, g - 1], q_r.at[n, g - 1], at(dy=dy))

    def q_wait(n, g):
        arrived(QA.at[pl.ds(4 * ym(-steps_y[n]) + 2 * (g - 1), 2)], q_s.at[n, g - 1], q_r.at[n, g - 1])

    def new_kv():
        out = project(y, 0)
        key = turned(out[:, :HEAD], kg[...], y)
        val = out[:, HEAD:].astype(jnp.bfloat16)
        KN[zp] = key
        VN[zp] = val
        nk[...] = key
        nv[...] = val
        send(KN.at[zp], KN.at[zp], kv_s.at[2], kv_r.at[2], pair)
        send(VN.at[zp], VN.at[zp], kv_s.at[3], kv_r.at[3], pair)

    def arrange_keys():
        b = trajectory(y)
        count = counts[b]
        first = jnp.broadcast_to(KN[0, 0:1, :].astype(jnp.float32), (BLOCK, HEAD))

        def put(at_row, on, k, v):
            on = jnp.full((BLOCK, HEAD), on, jnp.int32) > 0
            KM[pl.ds(at_row, BLOCK), :] = jnp.where(on, k.astype(jnp.float32), first).astype(jnp.bfloat16)
            VM[pl.ds(at_row, BLOCK), 0:HEAD] = jnp.where(on, v.astype(jnp.float32), 0.0).astype(jnp.bfloat16)
            VM[pl.ds(at_row, BLOCK), HEAD : 2 * HEAD] = jnp.where(on, 1.0, 0.0).astype(jnp.bfloat16)

        for s in range(SLOTS):
            on = jnp.int32(0)
            for j in range(SLOTS):
                hit = jnp.where(place[b, j] == s, 1, 0) * jnp.where(j < count, 1, 0)
                on = jnp.maximum(on, hit)
            rows = pl.ds(s % 8 * BLOCK, BLOCK)
            put(s * BLOCK, on, KC[s // 8, rows, :], VC[s // 8, rows, :])
        for s in range(2):
            rows = pl.ds(s * BLOCK, BLOCK)
            put(CACHE + s * BLOCK, zp, KN[1 - zp, rows, :], VN[1 - zp, rows, :])
            put(CACHE + TOK + s * BLOCK, jnp.int32(1), KN[zp, rows, :], VN[zp, rows, :])

    def attend(first_head, number):
        def body(n, carry):
            h = first_head + n
            s = lax.dot_general(QA[h], KM[...], (((1,), (1,)), ((), ())), preferred_element_type=jnp.float32)
            s_own = s[:, CACHE + TOK :] + TRI[...]
            s_rest = s[:, : CACHE + TOK]
            top = jnp.maximum(
                jnp.max(s_rest, axis=-1, keepdims=True), jnp.max(s_own, axis=-1, keepdims=True)
            )
            w_rest = jnp.exp2((s_rest - top) * FACTOR).astype(jnp.bfloat16)
            w_own = jnp.exp2((s_own - top) * FACTOR).astype(jnp.bfloat16)
            mixed = jnp.dot(w_rest, VM[: CACHE + TOK], preferred_element_type=jnp.float32) + jnp.dot(
                w_own, VM[CACHE + TOK :], preferred_element_type=jnp.float32
            )
            O[h] = (mixed[:, :HEAD] / mixed[:, HEAD:]).astype(jnp.bfloat16)
            return carry

        lax.fori_loop(0, number, body, 0)
        for n in range(number):
            h = first_head + n
            copy = pltpu.make_async_copy(O.at[h], att.at[:, pl.ds(pl.multiple_of(h * HEAD, HEAD), HEAD)], out_sem.at[h])
            copy.start()
            written.append(copy)

    written = []

    for copy in local[:1]:
        copy.wait()
    a_step(1, 0)
    for copy in local[1:3]:
        copy.wait()
    b_step(0)
    tables(y)
    a_step(1, 1)
    b_step(1)
    send(ck, KC.at[zp], kv_s.at[0], kv_r.at[0], pair)
    send(cv, VC.at[zp], kv_s.at[1], kv_r.at[1], pair)
    row = lax.broadcasted_iota(jnp.int32, (TOK, TOK), 0)
    col = lax.broadcasted_iota(jnp.int32, (TOK, TOK), 1)
    TRI[...] = jnp.where(col <= row, 0.0, NEG)
    a_step(1, 2)
    b_step(2)
    a_step(1, 3)
    tables(ym(1))
    a_step(1, 4)
    local[3].wait()
    a_step(2, 0)
    tables(ym(-1))
    b_step(3)
    for d in (0, 1):
        h_arrived(d, d)
        h_forward(d)
    a_step(1, 5)
    a_step(2, 1)
    b_step(4)
    tables(ym(2))
    a_step(2, 2)
    a_step(1, 6)
    for copy in local[4:]:
        copy.wait()
    h_from_core(y, 0)
    own_queries(1)
    a_step(2, 3)
    b_step(5)
    for d in (0, 1):
        h_arrived(d, 1 - d)
        h_to_core(ym(-1 if d == 0 else 1), 1 + d)
    a_step(2, 4)
    b_step(6)
    new_kv()
    for d in (0, 1):
        h_from_core(ym(-1 if d == 0 else 1), 1 + d)
    queries(ym(1), 1)
    q_send(0, 1)
    a_step(2, 5)
    queries(ym(-1), 1)
    q_send(1, 1)
    arrived(KC.at[1 - zp], kv_s.at[0], kv_r.at[0])
    arrived(VC.at[1 - zp], kv_s.at[1], kv_r.at[1])
    arrived(KN.at[1 - zp], kv_s.at[2], kv_r.at[2])
    arrived(VN.at[1 - zp], kv_s.at[3], kv_r.at[3])
    arrange_keys()
    for d in (0, 1):
        h_far_arrived(d)
        h_to_core(ym(2), 3 + d, half(d))
    attend(4 * y, 2)
    a_step(2, 6)
    queries(ym(1), 2)
    q_send(0, 2)
    queries(ym(-1), 2)
    q_send(1, 2)
    for d in (0, 1):
        h_from_core(ym(2), 3 + d, half(d))
    queries(ym(2), 1)
    q_send(2, 1)
    queries(ym(2), 2)
    q_send(2, 2)
    own_queries(2)
    attend(4 * y + 2, 2)
    for n in (0, 1):
        q_wait(n, 1)
        attend(4 * ym(-steps_y[n]), 2)
    for n in (0, 1):
        q_wait(n, 2)
        attend(4 * ym(-steps_y[n]) + 2, 2)
    for g in (1, 2):
        q_wait(2, g)
        attend(4 * ym(2) + 2 * (g - 1), 2)
    for copy in written:
        copy.wait()
    for copy in sent:
        copy.wait_send()


def on_device(hidden, w_query, key_weight, value_weight, q_gain, key_norm_gain, earlier_keys, earlier_values, counts, place):
    vmem = pl.BlockSpec(memory_space=pltpu.VMEM)
    smem = pl.BlockSpec(memory_space=pltpu.SMEM)
    hbm = pl.BlockSpec(memory_space=pl.ANY)
    bf16, f32 = jnp.bfloat16, jnp.float32
    dma = pltpu.SemaphoreType.DMA

    def both(*shape):
        return [dma(shape), dma(shape)]

    return pl.pallas_call(
        kernel,
        name="prefill",
        out_shape=(
            jax.ShapeDtypeStruct((TOK, 16 * HEAD), bf16),
            jax.ShapeDtypeStruct((TOK, HEAD), bf16),
            jax.ShapeDtypeStruct((TOK, HEAD), bf16),
        ),
        in_specs=[smem, smem, hbm, hbm, hbm, hbm, vmem, vmem, hbm, hbm],
        out_specs=(hbm, vmem, vmem),
        scratch_shapes=[
            pltpu.VMEM((NY, 2, TOK, 2048), bf16),
            pltpu.VMEM((3, NY, NX, NZ, 32, 256), bf16),
            pltpu.VMEM((2, 1024, HEAD), bf16),
            pltpu.VMEM((2, 1024, HEAD), bf16),
            pltpu.VMEM((2, TOK, HEAD), bf16),
            pltpu.VMEM((2, TOK, HEAD), bf16),
            pltpu.VMEM((KEYS, HEAD), bf16),
            pltpu.VMEM((KEYS, 2 * HEAD), bf16),
            pltpu.VMEM((NY, 4, TOK, HEAD), bf16),
            pltpu.VMEM((16, TOK, HEAD), bf16),
            pltpu.VMEM((NY, TOK, HEAD), f32),
            pltpu.VMEM((NY, TOK, HEAD), f32),
            pltpu.VMEM((TOK, TOK), f32),
            pltpu.VMEM((16, TOK, HEAD), bf16),
            dma((7,)),
            dma((16,)),
            *both(3, 4),
            *both(3, 2),
            *both(5),
            *both(4),
            *both(2, 2, 4),
            *both(2, 3, 8),
            *both(4),
            *both(4, 2, 4),
            *both(3, 2),
        ],
        compiler_params=pltpu.CompilerParams(
            collective_id=0, has_side_effects=True, vmem_limit_bytes=52 << 20
        ),
    )(
        counts,
        place,
        hidden,
        w_query,
        key_weight,
        value_weight,
        q_gain.reshape(1, HEAD),
        key_norm_gain.reshape(1, HEAD),
        earlier_keys,
        earlier_values,
    )


def solution(mesh):
    placed = (
        P("ctx", "tp"),
        P("ctx", "tp"),
        P("ctx", "tp"),
        P("ctx", "tp"),
        P(),
        P(),
        P("ctx", "tp"),
        P("ctx", "tp"),
        P(),
        P(),
    )
    return jax.shard_map(
        on_device,
        mesh=mesh,
        in_specs=placed,
        out_specs=(P("ctx", "tp"), P("ctx", "tp"), P("ctx", "tp")),
        check_vma=False,
    )
```

time: 451 us -> 110 us (0.24)
  waiting for transfers between devices: 358 us -> 0 us
  Pallas kernels: 0 us -> 102 us
  matrix products: 29.2 us -> 0 us
  other arithmetic: 27.5 us -> 0 us
  between operations: 14.7 us -> 0.72 us
  local copies, waits for them, and re-layouts: 15.7 us -> 5.86 us
  starting transfers between devices: 4.99 us -> 0 us
    all_gather x4 -> x0, waiting for transfers between devices: 350 us -> none  [the longest x1 142 us: on_device(): query = add_rows(lax.all_gather(w_query, 'ctx', axis=0, tiled=True))]
    pallas_call x0 -> x1, Pallas kernels: none -> 102 us  [on_device(): pl.pallas_call(kernel, name='prefill', out_shape=(jax.ShapeDtypeStruct((T...]
    dot_general x19 -> x0, matrix products: 29.2 us -> none  [the longest x3 13.1 us: add_rows(): return jnp.dot(whole, piece, preferred_element_type=jnp.float32)]
    reduce_sum x9 -> x0, other arithmetic: 7.41 us -> none  [the longest x8 6.8 us: attend(): total = jnp.sum(weight, axis=-1, keepdims=True)]
    dynamic_slice x10 -> x0, local copies, waits for them, and re-layouts: 6.11 us -> none  [the longest x8 4.69 us: on_device(): result = lax.map(attend, (query_rows, starts))]
    ppermute x4 -> x0, waiting for transfers between devices: 5.59 us -> none  [from_partner(): return lax.ppermute(value, axis, pairs)]
    add x8 -> x0, other arithmetic: 5.24 us -> none  [attend(): own_pos = lax.axis_index('ctx') % 2 * tok_rows + token]
    ppermute x4 -> x0, starting transfers between devices: 4.84 us -> none  [from_partner(): return lax.ppermute(value, axis, pairs)]
  transfers between devices with their start and end apart: 8 -> 0, of which waited for: 6 -> 0; matrix products, arithmetic and copies ran while one was open for 5% -> 0% of each run, Pallas kernels for 0% -> 0%
where the time goes in v1:
time: 110 us; the launch traced here: 109 us
  Pallas kernels  102 us (93%)
  local copies, waits for them, and re-layouts  5.86 us (5%)
    pallas_call x1, Pallas kernels, on_device(): pl.pallas_call(kernel, name='prefill', out_shape=(jax.ShapeDtypeStruct((T...  102 us
    unnamed x20, local copies, waits for them, and re-layouts  5.86 us

profile of v1, /device:TPU:1, one launch (start us, length us, event | category | flops | bytes accessed | tf_op | source)
XLA Modules:
  0.0 108.5 jit_solution(3752995234463964780)
XLA Ops:
  0.6 0.0 copy-start.3
  0.6 0.0 copy-start.4
  0.7 0.0 copy-start.5
  0.7 0.0 copy-start.6
  0.7 0.0 copy-start.7
  0.7 0.8 copy.13.place
  1.5 0.0 copy-done.3
  1.5 0.0 copy-done.4
  1.5 0.0 copy-done.5
  1.5 0.0 copy-done.6
  1.5 0.0 copy-done.7
  1.5 0.0 copy-start
  1.5 0.9 copy-done
  2.5 0.0 copy-start.1
  2.5 0.9 copy-done.1
  3.4 0.0 copy-start.2
  3.4 0.9 copy-done.2
  4.3 102.0 %prefill.1 = (bf16[256,2048]{1,0:T(8,128)(2,1)S(1)}, bf16[256,128]{1,0:T(8,128)(2,1)S(1)}, bf16[256,128]{1,0:T(8,128)(2,1)S(1)}) custom-call(s32[64]{0:T(128)S(1)} %copy-done.5, s32[64,16]{1,0:T(8,128)S(1)} %copy.13.place, bf16[256,2048]{1,0:T(8,128)(2,1)} %hid.1, bf16[32,2048]{1,0:T(8,128)(2,1)S(1)} %copy-done.2, bf16[32,128]{1,0:T(8,128)(2,1)S(1)} %copy-done.3, ...), custom_call_target="tpu_custom_call" | custom-call | tf_op jit(solution)/shard_map/prefill/pallas_call | solution.py:425
  106.3 1.0 copy.17
  107.3 0.6 copy.18
  107.9 0.6 copy.19
Async XLA Ops:
  0.6 0.9 copy-start.3
  0.6 0.9 copy-start.4
  0.7 0.9 copy-start.5
  0.7 0.9 copy-start.6
  0.7 0.9 copy-start.7
  1.5 1.0 copy-start
  2.5 0.9 copy-start.1
  3.4 0.9 copy-start.2

commit v2 on v1

v2 whole, which is shorter than its diff:
```python
import functools
import math

import jax
import jax.numpy as jnp
from jax import lax
from jax.experimental import pallas as pl
from jax.experimental.pallas import tpu as pltpu
from jax.sharding import PartitionSpec as P

MESH = pl.DeviceIdType.MESH
HEAD = 128
BLOCK = 128
TOK = 256
NY, NX, NZ = 4, 4, 8
SLOTS = 16
CACHE = SLOTS * BLOCK
KEYS = CACHE + 2 * TOK
FACTOR = HEAD**-0.5 * math.log2(math.e)
NEG = -1e30


def kernel(
    counts_in, place_in, hid, wq, kw, vw, qg_in, kg_in, ck, cv,
    att, nk, nv,
    H, W, W0, KVW, KC, VC, NEW, PB, KM, VM, QS, QA, COS, SIN, TRI, O, counts, place, qg, kg,
    local_sem, out_sem,
    p0_s, p0_r, h_s, h_r, c_s, c_r, kv_s, kv_r, za_s, za_r, xa_s, xa_r, xb_s, xb_r, zb_s, zb_r, q_s, q_r,
):
    i = lax.axis_index("ctx")
    c = lax.axis_index("tp")
    y, x, z = i // (NX * NZ), (i // NZ) % NX, i % NZ
    zp = z % 2
    kind = y % 2
    toward = 1 - 2 * kind
    sent = []

    def ym(k):
        return (y + k + NY) % NY

    def xm(k):
        return (x + k + NX) % NX

    def zm(k):
        return (z + k + NZ) % NZ

    def at(dy=0, dx=0, dz=0):
        return (ym(dy) * (NX * NZ) + xm(dx) * NZ + zm(dz), c)

    other_core = (i, 1 - c)
    pair = (i + 1 - 2 * zp, c)

    def send(src, dst, s, r, device):
        copy = pltpu.make_async_remote_copy(
            src_ref=src, dst_ref=dst, send_sem=s, recv_sem=r, device_id=device, device_id_type=MESH
        )
        copy.start()
        sent.append(copy)

    def arrived(dst, s, r):
        pltpu.make_async_remote_copy(
            src_ref=dst, dst_ref=dst, send_sem=s, recv_sem=r, device_id=other_core, device_id_type=MESH
        ).wait_recv()

    local = {}

    def bring(name, src, dst):
        copy = pltpu.make_async_copy(src, dst, local_sem.at[len(local)])
        copy.start()
        local[name] = copy

    def columns(yb, g):
        return pl.ds(pl.multiple_of(yb * 512 + (g - 1) * 256, 256), 256)

    bring("kw", kw, KVW.at[0])
    bring("vw", vw, KVW.at[1])
    bring("w1", wq.at[:, columns(y, 1)], W.at[0, y, x, z])
    bring("w2", wq.at[:, columns(y, 2)], W.at[1, y, x, z])
    bring("counts", counts_in, counts)
    bring("place", place_in, place)
    bring("qg", qg_in, qg)
    bring("kg", kg_in, kg)
    bring("hid", hid, H.at[y, c])
    bring("ck", ck, KC.at[zp])
    bring("cv", cv, VC.at[zp])

    barrier = pltpu.get_barrier_semaphore()
    for device in (at(dy=1), at(dy=-1), at(dy=2), at(dx=1), at(dx=-1), at(dz=1), at(dz=-1), other_core):
        pl.semaphore_signal(barrier, inc=1, device_id=device, device_id_type=MESH)
    pl.semaphore_wait(barrier, 8)

    steps_y = (1, -1, 2)

    def p0_queries(g):
        for n, dy in enumerate(steps_y):
            send(wq.at[:, columns(ym(dy), g)], W.at[g - 1, y, x, z], p0_s.at[n, g], p0_r.at[n, g], at(dy=dy))

    def p0_kv():
        for n, dy in enumerate(steps_y):
            send(KVW.at[ym(dy) % 2], W0.at[y, x, z], p0_s.at[n, 0], p0_r.at[n, 0], at(dy=dy))

    p0_queries(1)
    local["kw"].wait()
    local["vw"].wait()
    p0_kv()
    p0_queries(2)

    def own_rows(g):
        for n, dy in enumerate(steps_y):
            ref = W0.at[ym(-dy), x, z] if g == 0 else W.at[g - 1, ym(-dy), x, z]
            arrived(ref, p0_s.at[n, g], p0_r.at[n, g])

    def half(n):
        return pl.ds(128 * n, 128)

    def quarter(n):
        return pl.ds(64 * n, 64)

    for n in (0, 1):
        send(hid.at[half(n)], H.at[y, c, half(n)], h_s.at[0, n], h_r.at[0, n], at(dy=1))
        send(hid.at[half(1 - n)], H.at[y, c, half(1 - n)], h_s.at[1, 1 - n], h_r.at[1, 1 - n], at(dy=-1))
    send(hid, H.at[y, c], c_s.at[0], c_r.at[0], other_core)

    def side(d):
        return ym(-1 if d == 0 else 1)

    def h_arrived(d, n):
        arrived(H.at[side(d), c, half(n)], h_s.at[d, n], h_r.at[d, n])

    def h_forward(n):
        for d in (0, 1):
            ref = H.at[side(d), c, quarter(2 * d + n)]
            send(ref, ref, h_s.at[2, 2 * d + n], h_r.at[2, 2 * d + n], at(dy=1 if d == 0 else -1))

    def h_far(n):
        for d in (0, 1):
            ref = H.at[ym(2), c, quarter(2 * d + n)]
            arrived(ref, h_s.at[2, 2 * d + n], h_r.at[2, 2 * d + n])
            send(ref, ref, c_s.at[3 + 2 * d + n], c_r.at[3 + 2 * d + n], other_core)

    def h_far_from_core():
        for n in range(4):
            arrived(H.at[ym(2), 1 - c, quarter(n)], c_s.at[3 + n], c_r.at[3 + n])

    def h_to_core(d):
        send(H.at[side(d), c], H.at[side(d), c], c_s.at[1 + d], c_r.at[1 + d], other_core)

    def h_from_core(yb, slot):
        arrived(H.at[yb, 1 - c], c_s.at[slot], c_r.at[slot])

    def order(j):
        return zm((0, -1, 1, -2, 2, -3, 3, 4)[j])

    def a_block(g, xx, zz, hop=1, d=0):
        ref = W0 if g == 0 else W.at[g - 1]
        if hop == 4:
            return ref.at[pl.ds(2 * d, 2), xx, zz]
        return ref.at[:, xx, zz]

    def a_zsend(g, d, hop):
        sign = 1 - 2 * d
        ref = a_block(g, x, zm(-sign * (hop - 1)), hop, d)
        send(ref, ref, za_s.at[g - 1, d, hop - 1], za_r.at[g - 1, d, hop - 1], at(dz=sign))

    def a_zwait(g, d, hop):
        sign = 1 - 2 * d
        arrived(a_block(g, x, zm(-sign * hop), hop, d), za_s.at[g - 1, d, hop - 1], za_r.at[g - 1, d, hop - 1])

    def a_xsend(g, *blocks):
        for j in blocks:
            for d in (0, 1):
                ref = a_block(g, x, order(j))
                send(ref, ref, xa_s.at[g - 1, d, j], xa_r.at[g - 1, d, j], at(dx=1 - 2 * d))

    def a_xwait(g, d, j):
        arrived(a_block(g, xm(2 * d - 1), order(j)), xa_s.at[g - 1, d, j], xa_r.at[g - 1, d, j])

    def a_xforward(g, *blocks):
        for j in blocks:
            d = j % 2
            a_xwait(g, d, j)
            ref = a_block(g, xm(2 * d - 1), order(j))
            send(ref, ref, xa_s.at[g - 1, 2, j], xa_r.at[g - 1, 2, j], at(dx=1 - 2 * d))

    def a_z(g, n):
        if n == 0:
            own_rows(g)
        for d in (0, 1):
            if n:
                a_zwait(g, d, n)
            if n < 4:
                a_zsend(g, d, n + 1)

    def a_end(g):
        for j in range(8):
            a_xwait(g, 1 - j % 2, j)
            arrived(a_block(g, xm(2), order(j)), xa_s.at[g - 1, 2, j], xa_r.at[g - 1, 2, j])

    far = (0, -1, 1, 2)

    def b_zsend(n, hop):
        for d in (0, 1):
            sign = 1 - 2 * d
            ref = a_block(0, xm(far[n]), zm(-sign * (hop - 1)), hop, d)
            send(ref, ref, zb_s.at[n, d, hop - 1], zb_r.at[n, d, hop - 1], at(dz=sign))

    def b_zwait(n, hop):
        for d in (0, 1):
            sign = 1 - 2 * d
            arrived(a_block(0, xm(far[n]), zm(-sign * hop), hop, d), zb_s.at[n, d, hop - 1], zb_r.at[n, d, hop - 1])

    def b_step(n):
        if n == 0:
            own_rows(0)
            for d in (0, 1):
                ref = a_block(0, x, z)
                send(ref, ref, xb_s.at[d], xb_r.at[d], at(dx=1 - 2 * d))
            b_zsend(0, 1)
        elif n == 1:
            for d in (0, 1):
                arrived(a_block(0, xm(2 * d - 1), z), xb_s.at[d], xb_r.at[d])
                ref = a_block(0, xm(2 * d - 1), z, 4, d)
                send(ref, ref, xb_s.at[2 + d], xb_r.at[2 + d], at(dx=1 - 2 * d))
            b_zsend(1, 1)
            b_zsend(2, 1)
        elif n == 2:
            for d in (0, 1):
                arrived(a_block(0, xm(2), z, 4, d), xb_s.at[2 + d], xb_r.at[2 + d])
            b_zsend(3, 1)
        elif n <= 5:
            for m in range(4):
                b_zwait(m, n - 2)
                b_zsend(m, n - 1)
        else:
            for m in range(4):
                b_zwait(m, 4)

    def trajectory(yb):
        return (yb * (NX * NZ) + x * NZ + z) // 2

    def tables(yb):
        lane = lax.broadcasted_iota(jnp.int32, (TOK, HEAD), 1)
        freq = jnp.exp((lane % 64).astype(jnp.float32) * (-2.0 / HEAD) * math.log(1000000.0))
        start = counts[trajectory(yb)] * BLOCK + zp * TOK
        pos = (start + lax.broadcasted_iota(jnp.int32, (TOK, HEAD), 0)).astype(jnp.float32)
        angle = pos * freq
        COS[yb] = jnp.cos(angle)
        SIN[yb] = jnp.where(lane < 64, -1.0, 1.0) * jnp.sin(angle)

    def turned(v, gain, yb):
        v = v * lax.rsqrt(jnp.mean(v * v, axis=-1, keepdims=True) + 1e-06) * gain
        return (v * COS[yb] + pltpu.roll(v, 64, 1) * SIN[yb]).astype(jnp.bfloat16)

    def project(yb, w):
        rows, width = NY // 2 * NX * NZ * 32, w.shape[-1]
        low = jnp.dot(H[yb, 0], w[0:2].reshape(rows, width), preferred_element_type=jnp.float32)
        high = jnp.dot(H[yb, 1], w[2:4].reshape(rows, width), preferred_element_type=jnp.float32)
        return low + high

    def queries(yb, g):
        out = project(yb, W.at[g - 1])
        for h in (0, 1):
            QS[yb, 2 * (g - 1) + h] = turned(out[:, h * HEAD : (h + 1) * HEAD], qg[...], yb)

    def own_queries(g):
        queries(y, g)
        for h in (0, 1):
            QA[4 * y + 2 * (g - 1) + h] = QS[y, 2 * (g - 1) + h]

    def q_send(n, g):
        dy = steps_y[n]
        heads = pl.ds(2 * (g - 1), 2)
        send(QS.at[ym(dy), heads], QA.at[pl.ds(4 * y + 2 * (g - 1), 2)], q_s.at[n, g - 1], q_r.at[n, g - 1], at(dy=dy))

    def q_wait(n, g):
        arrived(QA.at[pl.ds(4 * ym(-steps_y[n]) + 2 * (g - 1), 2)], q_s.at[n, g - 1], q_r.at[n, g - 1])

    def fresh(yb):
        out = project(yb, W0)
        keys = jnp.full((TOK, HEAD), kind, jnp.int32) == 0
        return jnp.where(keys, turned(out, kg[...], yb).astype(jnp.float32), out).astype(jnp.bfloat16)

    def arrange_keys():
        b = trajectory(y)
        mine = lax.broadcasted_iota(jnp.int32, (SLOTS, 64), 1) == b
        slot_order = jnp.sum(jnp.where(mine, place[...].astype(jnp.float32), 0.0), axis=1, keepdims=True)
        used = lax.broadcasted_iota(jnp.int32, (SLOTS, 1), 0) < counts[b]
        first = jnp.broadcast_to(NEW[0, 0, 0:1, :].astype(jnp.float32), (BLOCK, HEAD))

        def put(at_row, on, k, v):
            KM[pl.ds(at_row, BLOCK), :] = jnp.where(on, k.astype(jnp.float32), first).astype(jnp.bfloat16)
            VM[pl.ds(at_row, BLOCK), 0:HEAD] = jnp.where(on, v.astype(jnp.float32), 0.0).astype(jnp.bfloat16)
            VM[pl.ds(at_row, BLOCK), HEAD : 2 * HEAD] = jnp.where(on, 1.0, 0.0).astype(jnp.bfloat16)

        for s in range(SLOTS):
            hit = jnp.where(used, jnp.where(slot_order == s, 1.0, 0.0), 0.0)
            on = jnp.broadcast_to(jnp.max(hit, axis=0, keepdims=True), (BLOCK, HEAD)) > 0.5
            rows = pl.ds(s % 8 * BLOCK, BLOCK)
            put(s * BLOCK, on, KC[s // 8, rows, :], VC[s // 8, rows, :])
        for s in range(2):
            rows = pl.ds(s * BLOCK, BLOCK)
            seen = jnp.full((BLOCK, HEAD), zp, jnp.int32) > 0
            put(CACHE + s * BLOCK, seen, NEW[0, 1 - zp, rows, :], NEW[1, 1 - zp, rows, :])
            put(CACHE + TOK + s * BLOCK, seen | True, NEW[0, zp, rows, :], NEW[1, zp, rows, :])

    def attend(*heads):
        scores = []
        for h in heads:
            s = lax.dot_general(QA[h], KM[...], (((1,), (1,)), ((), ())), preferred_element_type=jnp.float32)
            s_own = s[:, CACHE + TOK :] + TRI[...]
            s_rest = s[:, : CACHE + TOK]
            top = jnp.maximum(jnp.max(s_rest, axis=-1, keepdims=True), jnp.max(s_own, axis=-1, keepdims=True))
            scores.append((s_rest, s_own, top))
        for h, (s_rest, s_own, top) in zip(heads, scores):
            w_rest = jnp.exp2((s_rest - top) * FACTOR).astype(jnp.bfloat16)
            w_own = jnp.exp2((s_own - top) * FACTOR).astype(jnp.bfloat16)
            mixed = jnp.dot(w_rest, VM[: CACHE + TOK], preferred_element_type=jnp.float32) + jnp.dot(
                w_own, VM[CACHE + TOK :], preferred_element_type=jnp.float32
            )
            O[h] = (mixed[:, :HEAD] / mixed[:, HEAD:]).astype(jnp.bfloat16)
        for h in heads:
            written(h).start()

    def written(h):
        return pltpu.make_async_copy(O.at[h], att.at[:, pl.ds(pl.multiple_of(h * HEAD, HEAD), HEAD)], out_sem.at[h])

    local["w1"].wait()
    a_z(1, 0)
    a_xsend(1, 0)
    local["w2"].wait()
    a_z(2, 0)
    W0[y, x, z] = KVW[kind]
    b_step(0)
    for name in ("counts", "place", "qg", "kg"):
        local[name].wait()
    a_z(1, 1)
    a_xsend(1, 1, 2)
    a_z(2, 1)
    a_xforward(1, 0)
    b_step(1)
    tables(y)
    a_z(1, 2)
    a_xsend(1, 3, 4)
    a_z(2, 2)
    a_xforward(1, 1, 2)
    b_step(2)
    tables(ym(1))
    a_z(1, 3)
    a_xsend(1, 5, 6)
    a_z(2, 3)
    a_xforward(1, 3, 4)
    b_step(3)
    tables(ym(-1))
    a_z(1, 4)
    a_xsend(1, 7)
    a_z(2, 4)
    b_step(4)
    a_xforward(1, 5, 6)
    a_xsend(2, 0, 1, 2, 3)
    tables(ym(2))
    for d in (0, 1):
        h_arrived(d, d)
    b_step(5)
    a_xforward(1, 7)
    a_xsend(2, 4, 5, 6, 7)
    row = lax.broadcasted_iota(jnp.int32, (TOK, TOK), 0)
    col = lax.broadcasted_iota(jnp.int32, (TOK, TOK), 1)
    TRI[...] = jnp.where(col <= row, 0.0, NEG)
    send(ck, KC.at[zp], kv_s.at[0], kv_r.at[0], pair)
    send(cv, VC.at[zp], kv_s.at[1], kv_r.at[1], pair)
    b_step(6)
    for d in (0, 1):
        h_arrived(d, 1 - d)
        h_to_core(d)
    h_forward(0)
    a_end(1)
    for name in ("hid", "ck", "cv"):
        local[name].wait()
    h_from_core(y, 0)
    own_queries(1)
    NEW[kind, zp] = fresh(y)
    for d in (0, 1):
        h_from_core(side(d), 1 + d)
    PB[...] = fresh(ym(toward))
    send(PB, NEW.at[kind, zp], kv_s.at[4], kv_r.at[4], at(dy=toward))
    a_xforward(2, 0, 1)
    queries(ym(1), 1)
    q_send(0, 1)
    a_xforward(2, 2, 3)
    queries(ym(-1), 1)
    q_send(1, 1)
    h_forward(1)
    a_xforward(2, 4, 5)
    arrived(NEW.at[1 - kind, zp], kv_s.at[4], kv_r.at[4])
    for n in (0, 1):
        send(NEW.at[n, zp], NEW.at[n, zp], kv_s.at[2 + n], kv_r.at[2 + n], pair)
    nk[...] = NEW[0, zp]
    nv[...] = NEW[1, zp]
    a_xforward(2, 6, 7)
    h_far(0)
    arrived(KC.at[1 - zp], kv_s.at[0], kv_r.at[0])
    arrived(VC.at[1 - zp], kv_s.at[1], kv_r.at[1])
    for n in (0, 1):
        arrived(NEW.at[n, 1 - zp], kv_s.at[2 + n], kv_r.at[2 + n])
    arrange_keys()
    q_wait(0, 1)
    attend(4 * y, 4 * y + 1, 4 * ym(-1), 4 * ym(-1) + 1)
    h_far(1)
    a_end(2)
    queries(ym(1), 2)
    q_send(0, 2)
    queries(ym(-1), 2)
    q_send(1, 2)
    h_far_from_core()
    queries(ym(2), 1)
    q_send(2, 1)
    queries(ym(2), 2)
    q_send(2, 2)
    own_queries(2)
    q_wait(1, 1)

    def four(n, carry):
        @pl.when(n == 1)
        def _():
            q_wait(0, 2)
            q_wait(1, 2)

        @pl.when(n == 2)
        def _():
            q_wait(2, 1)
            q_wait(2, 2)

        a = 4 * ((y + 1 + 2 * n - 3 * (n // 2)) % NY) + 2 * (n % 2)
        b = 4 * ((y + n) % NY) + 2
        attend(a, a + 1, b, b + 1)
        return carry

    lax.fori_loop(0, 3, four, 0)
    for h in range(4 * NY):
        written(h).wait()
    for copy in sent:
        copy.wait_send()


def on_device(hidden, w_query, key_weight, value_weight, q_gain, key_norm_gain, earlier_keys, earlier_values, counts, place):
    vmem = pl.BlockSpec(memory_space=pltpu.VMEM)
    hbm = pl.BlockSpec(memory_space=pltpu.HBM)
    bf16, f32 = jnp.bfloat16, jnp.float32
    dma = pltpu.SemaphoreType.DMA

    def both(*shape):
        return [dma(shape), dma(shape)]

    return pl.pallas_call(
        kernel,
        name="prefill",
        out_shape=(
            jax.ShapeDtypeStruct((TOK, 16 * HEAD), bf16),
            jax.ShapeDtypeStruct((TOK, HEAD), bf16),
            jax.ShapeDtypeStruct((TOK, HEAD), bf16),
        ),
        in_specs=[hbm] * 10,
        out_specs=(hbm, vmem, vmem),
        scratch_shapes=[
            pltpu.VMEM((NY, 2, TOK, 2048), bf16),
            pltpu.VMEM((2, NY, NX, NZ, 32, 256), bf16),
            pltpu.VMEM((NY, NX, NZ, 32, HEAD), bf16),
            pltpu.VMEM((2, 32, HEAD), bf16),
            pltpu.VMEM((2, 1024, HEAD), bf16),
            pltpu.VMEM((2, 1024, HEAD), bf16),
            pltpu.VMEM((2, 2, TOK, HEAD), bf16),
            pltpu.VMEM((TOK, HEAD), bf16),
            pltpu.VMEM((KEYS, HEAD), bf16),
            pltpu.VMEM((KEYS, 2 * HEAD), bf16),
            pltpu.VMEM((NY, 4, TOK, HEAD), bf16),
            pltpu.VMEM((16, TOK, HEAD), bf16),
            pltpu.VMEM((NY, TOK, HEAD), f32),
            pltpu.VMEM((NY, TOK, HEAD), f32),
            pltpu.VMEM((TOK, TOK), f32),
            pltpu.VMEM((16, TOK, HEAD), bf16),
            pltpu.SMEM((64,), jnp.int32),
            pltpu.VMEM((SLOTS, 64), jnp.int32),
            pltpu.VMEM((1, HEAD), f32),
            pltpu.VMEM((1, HEAD), f32),
            dma((11,)),
            dma((16,)),
            *both(3, 3),
            *both(3, 4),
            *both(7),
            *both(5),
            *both(2, 2, 4),
            *both(2, 3, 8),
            *both(4),
            *both(4, 2, 4),
            *both(3, 2),
        ],
        compiler_params=pltpu.CompilerParams(
            collective_id=0, has_side_effects=True, vmem_limit_bytes=52 << 20
        ),
    )(
        *(
            pltpu.with_memory_space_constraint(a, pltpu.HBM)
            for a in (
                counts,
                place.T,
                hidden,
                w_query,
                key_weight,
                value_weight,
                q_gain.reshape(1, HEAD),
                key_norm_gain.reshape(1, HEAD),
                earlier_keys,
                earlier_values,
            )
        )
    )


def solution(mesh):
    placed = (
        P("ctx", "tp"),
        P("ctx", "tp"),
        P("ctx", "tp"),
        P("ctx", "tp"),
        P(),
        P(),
        P("ctx", "tp"),
        P("ctx", "tp"),
        P(),
        P(),
    )
    return jax.shard_map(
        on_device,
        mesh=mesh,
        in_specs=placed,
        out_specs=(P("ctx", "tp"), P("ctx", "tp"), P("ctx", "tp")),
        check_vma=False,
    )
```

time: 110 us -> 81.9 us (0.74)
  Pallas kernels: 102 us -> 77.7 us
  local copies, waits for them, and re-layouts: 5.86 us -> 2.23 us
    pallas_call x1, Pallas kernels: 102 us -> 77.7 us  [on_device(): pl.pallas_call(kernel, name='prefill', out_shape=(jax.ShapeDtypeStruct((T...]
    unnamed x20 -> x3, local copies, waits for them, and re-layouts: 5.86 us -> 2.23 us
where the time goes in v2:
time: 81.9 us; the launch traced here: 80.6 us
  Pallas kernels  77.7 us (95%)
  local copies, waits for them, and re-layouts  2.23 us (3%)
    pallas_call x1, Pallas kernels, on_device(): pl.pallas_call(kernel, name='prefill', out_shape=(jax.ShapeDtypeStruct((T...  77.7 us
    unnamed x3, local copies, waits for them, and re-layouts  2.23 us

profile of v2, /device:TPU:1, one launch (start us, length us, event | category | flops | bytes accessed | tf_op | source)
XLA Modules:
  0.0 80.6 jit_solution(2530509523589949543)
XLA Ops:
  0.6 77.7 %prefill.1 = (bf16[256,2048]{1,0:T(8,128)(2,1)S(1)}, bf16[256,128]{1,0:T(8,128)(2,1)S(1)}, bf16[256,128]{1,0:T(8,128)(2,1)S(1)}) custom-call(s32[64]{0:T(128)} %counts_in.1, s32[16,64]{1,0:T(8,128)} %bitcast.3, bf16[256,2048]{1,0:T(8,128)(2,1)} %hid.1, bf16[32,2048]{1,0:T(8,128)(2,1)} %wq.1, bf16[32,128]{1,0:T(8,128)(2,1)} %kw.1, bf16[32,128]{1,0:T(8,128)(2,1)} %vw.1, ...), custom_call_target="tpu_custom_call" | custom-call | tf_op jit(solution)/shard_map/prefill/pallas_call | solution.py:454
  78.3 1.0 %copy.16 = bf16[256,2048]{1,0:T(8,128)(2,1)} copy(bf16[256,2048]{1,0:T(8,128)(2,1)S(1)} %get-tuple-element.6) | data formatting | bytes 2097152
  79.3 0.6 copy.17
  79.9 0.6 copy.18

commit v3 on v2

--- a/solution.py
+++ b/solution.py
@@ -360,6 +360,8 @@
     tables(ym(2))
     for d in (0, 1):
         h_arrived(d, d)
+    h_forward(0)
+    h_forward(1)
     b_step(5)
     a_xforward(1, 7)
     a_xsend(2, 4, 5, 6, 7)
@@ -372,7 +374,6 @@
     for d in (0, 1):
         h_arrived(d, 1 - d)
         h_to_core(d)
-    h_forward(0)
     a_end(1)
     for name in ("hid", "ck", "cv"):
         local[name].wait()
@@ -389,7 +390,6 @@
     a_xforward(2, 2, 3)
     queries(ym(-1), 1)
     q_send(1, 1)
-    h_forward(1)
     a_xforward(2, 4, 5)
     arrived(NEW.at[1 - kind, zp], kv_s.at[4], kv_r.at[4])
     for n in (0, 1):

time: 81.9 us -> 77.7 us (0.949)
  Pallas kernels: 77.7 us -> 74.2 us
    pallas_call x1, Pallas kernels: 77.7 us -> 74.2 us  [on_device(): pl.pallas_call(kernel, name='prefill', out_shape=(jax.ShapeDtypeStruct((T...]
where the time goes in v3:
time: 77.7 us; the launch traced here: 77 us
  Pallas kernels  74.2 us (95%)
  local copies, waits for them, and re-layouts  2.23 us (3%)
    pallas_call x1, Pallas kernels, on_device(): pl.pallas_call(kernel, name='prefill', out_shape=(jax.ShapeDtypeStruct((T...  74.2 us
    unnamed x3, local copies, waits for them, and re-layouts  2.23 us

profile of v3, /device:TPU:1, one launch (start us, length us, event | category | flops | bytes accessed | tf_op | source)
XLA Modules:
  0.0 77.0 jit_solution(14282339768754175511)
XLA Ops:
  0.6 74.2 %prefill.1 = (bf16[256,2048]{1,0:T(8,128)(2,1)S(1)}, bf16[256,128]{1,0:T(8,128)(2,1)S(1)}, bf16[256,128]{1,0:T(8,128)(2,1)S(1)}) custom-call(s32[64]{0:T(128)} %counts_in.1, s32[16,64]{1,0:T(8,128)} %bitcast.3, bf16[256,2048]{1,0:T(8,128)(2,1)} %hid.1, bf16[32,2048]{1,0:T(8,128)(2,1)} %wq.1, bf16[32,128]{1,0:T(8,128)(2,1)} %kw.1, bf16[32,128]{1,0:T(8,128)(2,1)} %vw.1, ...), custom_call_target="tpu_custom_call" | custom-call | tf_op jit(solution)/shard_map/prefill/pallas_call | solution.py:454
  74.8 1.0 %copy.16 = bf16[256,2048]{1,0:T(8,128)(2,1)} copy(bf16[256,2048]{1,0:T(8,128)(2,1)S(1)} %get-tuple-element.6) | data formatting | bytes 2097152
  75.8 0.6 copy.17
  76.4 0.6 copy.18

commit v4 on v3

--- a/solution.py
+++ b/solution.py
@@ -22,7 +22,7 @@
 
 def kernel(
     counts_in, place_in, hid, wq, kw, vw, qg_in, kg_in, ck, cv,
-    att, nk, nv,
+    att, new,
     H, W, W0, KVW, KC, VC, NEW, PB, KM, VM, QS, QA, COS, SIN, TRI, O, counts, place, qg, kg,
     local_sem, out_sem,
     p0_s, p0_r, h_s, h_r, c_s, c_r, kv_s, kv_r, za_s, za_r, xa_s, xa_r, xb_s, xb_r, zb_s, zb_r, q_s, q_r,
@@ -394,8 +394,8 @@
     arrived(NEW.at[1 - kind, zp], kv_s.at[4], kv_r.at[4])
     for n in (0, 1):
         send(NEW.at[n, zp], NEW.at[n, zp], kv_s.at[2 + n], kv_r.at[2 + n], pair)
-    nk[...] = NEW[0, zp]
-    nv[...] = NEW[1, zp]
+    new[0] = NEW[0, zp]
+    new[1] = NEW[1, zp]
     a_xforward(2, 6, 7)
     h_far(0)
     arrived(KC.at[1 - zp], kv_s.at[0], kv_r.at[0])
@@ -451,16 +451,15 @@
     def both(*shape):
         return [dma(shape), dma(shape)]
 
-    return pl.pallas_call(
+    attended, new = pl.pallas_call(
         kernel,
         name="prefill",
         out_shape=(
             jax.ShapeDtypeStruct((TOK, 16 * HEAD), bf16),
-            jax.ShapeDtypeStruct((TOK, HEAD), bf16),
-            jax.ShapeDtypeStruct((TOK, HEAD), bf16),
+            jax.ShapeDtypeStruct((2, TOK, HEAD), bf16),
         ),
         in_specs=[hbm] * 10,
-        out_specs=(hbm, vmem, vmem),
+        out_specs=(hbm, vmem),
         scratch_shapes=[
             pltpu.VMEM((NY, 2, TOK, 2048), bf16),
             pltpu.VMEM((2, NY, NX, NZ, 32, 256), bf16),
@@ -514,6 +513,7 @@
             )
         )
     )
+    return attended, new[0], new[1]
 
 
 def solution(mesh):

time: 77.7 us -> 77.1 us (level)
    unnamed x3 -> x1, local copies, waits for them, and re-layouts: 2.23 us -> 0.97 us
where the time goes in v4:
time: 77.1 us; the launch traced here: 76.5 us
  Pallas kernels  74.2 us (96%)
  local copies, waits for them, and re-layouts  1.63 us (2%)
    pallas_call x1, Pallas kernels, on_device(): pl.pallas_call(kernel, name='prefill', out_shape=(jax.ShapeDtypeStruct((T...  74.2 us

profile of v4, /device:TPU:1, one launch (start us, length us, event | category | flops | bytes accessed | tf_op | source)
XLA Modules:
  0.0 76.5 jit_solution(6319995941253145497)
XLA Ops:
  0.6 74.2 %prefill.1 = (bf16[256,2048]{1,0:T(8,128)(2,1)S(1)}, bf16[2,256,128]{2,1,0:T(8,128)(2,1)S(1)}) custom-call(s32[64]{0:T(128)} %counts_in.1, s32[16,64]{1,0:T(8,128)} %bitcast.7, bf16[256,2048]{1,0:T(8,128)(2,1)} %hid.1, bf16[32,2048]{1,0:T(8,128)(2,1)} %wq.1, bf16[32,128]{1,0:T(8,128)(2,1)} %kw.1, bf16[32,128]{1,0:T(8,128)(2,1)} %vw.1, f32[1,128]{1,0:T(1,128)} %bitcast.8, ...), custom_call_target="tpu_custom_call" | custom-call | tf_op jit(solution)/shard_map/prefill/pallas_call | solution.py:454
  74.8 0.7 slice_bitcast_fusion
  75.5 1.0 %copy.14 = bf16[256,2048]{1,0:T(8,128)(2,1)} copy(bf16[256,2048]{1,0:T(8,128)(2,1)S(1)} %get-tuple-element.12) | data formatting | bytes 2097152
